TPU v7x, 256 devices: a whole 4x4x8 slice. The times are simulated.
256 devices in a mesh: dp: 8 (over y, core), expert: 32 (over x, z).
Axes of the slice: x: 4, y: 4, z: 8, core: 2. Of those that a mesh axis runs over, the one named last changes fastest.
Arguments:
- hidden_token_tiles: bfloat16 [8, 1024, 1024], P(None, 'dp'), may hold values from -6 to 6
- gradient_token_tiles: bfloat16 [8, 7168, 1024], P(None, 'expert', 'dp'), may hold values from -0.59765625 to 0.59765625
- momentum: float32 [8, 7168, 1024], P('dp', 'expert'), may hold values from -54 to 54, as said below
- filled_tile_count: int32 [8, 8], replicated, may hold values from 1 to 8, as said below
Outputs:
- new_momentum: float32 [8, 7168, 1024], P('dp', 'expert')
- update: float32 [8, 7168, 1024], P(None, 'expert')
Inputs may be any that keep to these rules, and one draw needn't show every extreme that they name: momentum entries are finite reals. filled_tile_count[g, x] filled tiles stand at the head of group g's slots for expert x; in every draw one expert is full in every group.
All inputs are finite; a program needn't handle non-finite values.
Results may differ from a plain program's by a relative error of at most 0.0009.
Values may be sent and summed in bfloat16 or wider, within the bound.
No kernel may reach another device: no remote copies, remote signals or barrier semaphores. Data moves between devices by JAX's collectives and lax.ppermute only.
A program may use at most 64 MiB of HBM per device.

v0:
```python
import math
import jax
import jax.numpy as jnp
from jax import lax
from jax.sharding import PartitionSpec as P

D = 7168
FF = 1024
TILE = 16
ITERS = 2
MOMENTUM_DECAY = 0.95
EPSILON = 1e-07
COEF_A = 3.4445
COEF_B = -4.775
COEF_C = 2.0315


def full_dot(left, right):
    return jnp.dot(left, right, precision=lax.Precision.HIGHEST, preferred_element_type=jnp.float32)


def body(hidden_token_tiles, gradient_token_tiles, momentum, filled_tile_count):
    group = lax.axis_index("dp")
    rows_group = hidden_token_tiles.shape[1]
    experts_here = hidden_token_tiles.shape[0]
    limits = lax.dynamic_index_in_dim(filled_tile_count, group, 0, keepdims=False) * TILE
    positions = lax.broadcasted_iota(jnp.int32, (experts_here, rows_group), 1)
    tallied_tiles = positions < limits[:, None]
    retained_entries = jnp.where(
        tallied_tiles[:, :, None], hidden_token_tiles, jnp.zeros((), jnp.bfloat16)
    )
    gradient = lax.psum_scatter(
        jnp.einsum(
            "tba,tan->tbn",
            gradient_token_tiles,
            retained_entries,
            preferred_element_type=jnp.float32,
        ),
        "dp",
        scatter_dimension=0,
        tiled=True,
    )[0]
    moment = MOMENTUM_DECAY * momentum[0] + gradient
    current = moment
    for iteration in range(ITERS):
        gram_total = lax.psum(full_dot(current.T, current).astype(jnp.bfloat16), "expert").astype(
            jnp.float32
        )
        if iteration == 0:
            factor = 1.0 / (jnp.sqrt(jnp.trace(gram_total)) + EPSILON)
            current = current * factor
            gram_total = gram_total * (factor * factor)
        mixer = COEF_B * gram_total + COEF_C * full_dot(gram_total, gram_total)
        current = COEF_A * current + full_dot(current, mixer)
    update_local = current * math.sqrt(max(FF, D))
    gathered = lax.all_gather(update_local[None], "dp", axis=0, tiled=True)
    return (moment[None], gathered)


def solution(mesh):
    placed = (P(None, "dp", None), P(None, "expert", "dp"), P("dp", "expert", None), P())
    return jax.shard_map(
        body,
        mesh=mesh,
        in_specs=placed,
        out_specs=(P("dp", "expert", None), P(None, "expert", None)),
        check_vma=False,
    )
```

profile of v0, /device:TPU:1, one launch (start us, length us, event | category | flops | bytes accessed | tf_op | source)
XLA Modules:
  0.0 476.9 jit_solution(4458757613890195179)
XLA Ops:
  7.2 0.0 copy-start
  7.2 0.0 reduce-scatter.2.cloned.1.call-start
  7.2 0.7 multiply_bitcast_fusion
  8.0 0.1 iota_compare_fusion.1
  8.0 0.2 copy-done
  8.2 5.8 %convolution_bitcast_fusion = f32[8,224,1024]{2,1,0:T(8,128)} fusion(bf16[8,224,128]{2,1,0:T(8,128)(2,1)S(1)} %copy-done, bf16[8,128,1024]{2,1,0:T(8,128)(2,1)} %param.4, pred[8,128]{1,0:T(8,128)(4,1)S(1)} %iota_compare_fusion.1), kind=kOutput, calls=%fused_computation.14 | convolution fusion | flops 470810624 | bytes 9896960 | tf_op jit(solution)/shard_map/tba,tan->tbn/dot_general | solution.py:33
  14.0 0.0 copy-start.4
  14.0 0.0 reduce-scatter.2.cloned.1.call-update
  14.0 0.0 all-reduce.3.cloned.1.call-start
  14.1 53.4 %reduce-scatter.2.cloned.1.call-done = f32[1,224,1024]{2,1,0:T(8,128)} async-done(((f32[8,224,1024]{2,1,0:T(8,128)}), f32[1,224,1024]{2,1,0:T(8,128)}) %reduce-scatter.2.cloned.1.call-update) | async-done | bytes 917520 | tf_op jit(solution)/shard_map/reduce_scatter | solution.py:32
  67.5 0.0 copy-done.4
  67.5 1.3 multiply_add_fusion
  68.8 0.0 copy-start.2
  68.8 4.8 %convolution_convert_fusion.1 = bf16[1024,1024]{1,0:T(8,128)(2,1)} fusion(f32[1,224,1024]{2,1,0:T(8,128)S(1)} %multiply_add_fusion), kind=kOutput, calls=%fused_computation.24 | convolution fusion | flops 2819620864 | bytes 3014656 | tf_op jit(solution)/shard_map/dot_general | solution.py:19
  73.6 0.0 all-reduce.3.cloned.1.call-update
  73.6 0.2 all-reduce.5.cloned.1.call-start
  73.9 149.9 %all-reduce.3.cloned.1.call-done = bf16[1024,1024]{1,0:T(8,128)(2,1)} async-done(((bf16[1024,1024]{1,0:T(8,128)(2,1)}), bf16[1024,1024]{1,0:T(8,128)(2,1)}) %all-reduce.3.cloned.1.call-update) | async-done | bytes 2097168 | tf_op jit(solution)/shard_map/psum | solution.py:46
  223.7 2.3 fusion.5
  226.8 0.0 copy-start.1
  226.8 16.3 %fusion = f32[1024,1024]{1,0:T(8,128)S(1)} fusion(bf16[1024,1024]{1,0:T(8,128)(2,1)} %all-reduce.3.cloned.1.call-done, f32[]{:T(128)S(6)} %mul.70), kind=kOutput, calls=%fused_computation.2 | convolution fusion | flops 12886999040 | bytes 6291460 | tf_op jit(solution)/shard_map/dot_general | solution.py:19
  243.2 0.0 copy-done.2
  243.2 0.0 copy-done.1
  243.2 4.1 fusion.23
  247.3 4.8 %convolution_convert_fusion = bf16[1024,1024]{1,0:T(8,128)(2,1)} fusion(f32[224,1024]{1,0:T(8,128)S(1)} %fusion.23), kind=kOutput, calls=%fused_computation.23 | convolution fusion | flops 2819620864 | bytes 3014656 | tf_op jit(solution)/shard_map/dot_general | solution.py:19
  252.1 0.0 all-reduce.5.cloned.1.call-update
  252.1 0.0 all-gather.3.cloned.1.call-start
  252.2 151.3 %all-reduce.5.cloned.1.call-done = bf16[1024,1024]{1,0:T(8,128)(2,1)} async-done(((bf16[1024,1024]{1,0:T(8,128)(2,1)}), bf16[1024,1024]{1,0:T(8,128)(2,1)}) %all-reduce.5.cloned.1.call-update) | async-done | bytes 2097168 | tf_op jit(solution)/shard_map/psum | solution.py:46
  403.5 0.0 copy-start.3
  403.5 4.7 fusion.39
  408.2 0.0 copy-done.3
  408.2 4.6 fusion.26
  412.9 0.0 all-gather.3.cloned.1.call-update
  412.9 50.0 %all-gather.3.cloned.1.call-done = f32[1792,1024]{1,0:T(8,128)} async-done(((f32[224,1024]{1,0:T(8,128)}), f32[1792,1024]{1,0:T(8,128)}) %all-gather.3.cloned.1.call-update) | async-done | bytes 7340048 | tf_op jit(solution)/shard_map/all_gather | solution.py:56
  462.9 7.5 %copy.9 = f32[8,224,1024]{2,1,0:T(8,128)} copy(f32[8,224,1024]{2,1,0:T(8,128)} %bitcast.20) | data formatting | bytes 14680064
Async XLA Ops:
  7.2 1.0 copy-start
  7.2 60.3 %reduce-scatter.2.cloned.1.call-start = ((), (), s32[]{:S(2)}) async-start(), calls=%async_computation.1 | async-start | bytes 8257536 | tf_op jit(solution)/shard_map/reduce_scatter | solution.py:32
  14.0 53.4 %copy-start.4 = (f32[1,224,1024]{2,1,0:T(8,128)S(1)}, f32[1,224,1024]{2,1,0:T(8,128)}, u32[]{:S(2)}) copy-start(f32[1,224,1024]{2,1,0:T(8,128)} %param.6) | copy-start | bytes 2752516
  14.0 209.7 %all-reduce.3.cloned.1.call-start = ((), (), s32[]{:S(2)}) async-start(), calls=%async_computation.2 | async-start | bytes 4194304 | tf_op jit(solution)/shard_map/psum | solution.py:46
  68.8 174.4 %copy-start.2 = (f32[1,224,1024]{2,1,0:T(8,128)}, f32[1,224,1024]{2,1,0:T(8,128)S(1)}, u32[]{:S(2)}) copy-start(f32[1,224,1024]{2,1,0:T(8,128)S(1)} %multiply_add_fusion) | copy-start | bytes 2752516
  73.6 329.9 %all-reduce.5.cloned.1.call-start = ((), (), s32[]{:S(2)}) async-start(), calls=%async_computation.3 | async-start | bytes 4194304 | tf_op jit(solution)/shard_map/psum | solution.py:46
  226.8 16.4 %copy-start.1 = (bf16[1024,1024]{1,0:T(8,128)(2,1)S(1)}, bf16[1024,1024]{1,0:T(8,128)(2,1)}, u32[]{:S(2)}) copy-start(bf16[1024,1024]{1,0:T(8,128)(2,1)} %all-reduce.3.cloned.1.call-done) | copy-start | bytes 6291460
  252.1 210.7 %all-gather.3.cloned.1.call-start = ((), (), s32[]{:S(2)}) async-start(), calls=%async_computation.4 | async-start | bytes 8257536 | tf_op jit(solution)/shard_map/all_gather | solution.py:56
  403.5 4.7 copy-start.3
Sparse Core Ops, SparseCore 0:
  14.2 53.2 reduce-scatter.1
  73.7 149.9 all-reduce.2
  252.2 151.2 all-reduce.4
  413.0 49.7 all-gather.2
where the time goes:
time: 477 us
  waiting for transfers between devices  405 us (85%)
  matrix products  45.2 us (9%)
  between operations  14.6 us (3%)
  local copies, waits for them, and re-layouts  7.71 us (2%)
    psum x2, waiting for transfers between devices, body(): lax.psum(full_dot(current.T, current).astype(jnp.bfloat16), 'expert')  301 us
    reduce_scatter x1, waiting for transfers between devices, body(): lax.psum_scatter(jnp.einsum('tba,tan->tbn', gradient_token_tiles, retaine...  53.4 us
    all_gather x1, waiting for transfers between devices, body(): gathered = lax.all_gather(update_local[None], 'dp', axis=0, tiled=True)  50 us
    dot_general x6, matrix products, full_dot(): jnp.dot(left, right, precision=lax.Precision.HIGHEST, preferred_element_t...  39.4 us
  transfers between devices with their start and end apart: 4, of which 4 were waited for; matrix products, arithmetic and copies ran while one was open for 0% of the time, Pallas kernels for 0%

commit v1 on v0

--- a/solution.py
+++ b/solution.py
@@ -1,3 +1,4 @@
+import functools
 import math
 import jax
 import jax.numpy as jnp
@@ -13,6 +14,16 @@
 COEF_A = 3.4445
 COEF_B = -4.775
 COEF_C = 2.0315
+
+
+def change_seats_all(matrix, chip_axis):
+    carry_in = jnp.stack([matrix for _ in range(jax.lax.axis_size(chip_axis))])
+    seen_now = jax.lax.all_to_all(carry_in, chip_axis, 0, 0)
+    w_next = jnp.concatenate(seen_now, axis=0)
+    return w_next
+
+
+open_halves = functools.partial(change_seats_all, chip_axis="dp")
 
 
 def full_dot(left, right):
@@ -53,7 +64,7 @@
         mixer = COEF_B * gram_total + COEF_C * full_dot(gram_total, gram_total)
         current = COEF_A * current + full_dot(current, mixer)
     update_local = current * math.sqrt(max(FF, D))
-    gathered = lax.all_gather(update_local[None], "dp", axis=0, tiled=True)
+    gathered = open_halves(update_local[None])
     return (moment[None], gathered)
 
 

time: 477 us -> 516 us (1.082)
  blocking collectives: 0 us -> 92.9 us
  waiting for transfers between devices: 405 us -> 355 us
    all_to_all x0 -> x1, blocking collectives: none -> 92.9 us  [change_seats_all(): seen_now = jax.lax.all_to_all(carry_in, chip_axis, 0, 0)]
    all_gather x1 -> x0, waiting for transfers between devices: 50 us -> none  [body(): gathered = lax.all_gather(update_local[None], 'dp', axis=0, tiled=True)]
  transfers between devices with their start and end apart: 4 -> 3, of which waited for: 4 -> 3; matrix products, arithmetic and copies ran while one was open for 0% -> 0% of each run, Pallas kernels for 0% -> 0%
where the time goes in v1:
time: 516 us; the launch traced here: 515 us
  waiting for transfers between devices  355 us (69%)
  blocking collectives  92.9 us (18%)
  matrix products  44.3 us (9%)
  between operations  14.6 us (3%)
    psum x2, waiting for transfers between devices, body(): lax.psum(full_dot(current.T, current).astype(jnp.bfloat16), 'expert')  301 us
    all_to_all x1, blocking collectives, change_seats_all(): seen_now = jax.lax.all_to_all(carry_in, chip_axis, 0, 0)  92.9 us
    reduce_scatter x1, waiting for transfers between devices, body(): lax.psum_scatter(jnp.einsum('tba,tan->tbn', gradient_token_tiles, retaine...  53.4 us
    dot_general x6, matrix products, full_dot(): jnp.dot(left, right, precision=lax.Precision.HIGHEST, preferred_element_t...  38.5 us
  transfers between devices with their start and end apart: 3, of which 3 were waited for; matrix products, arithmetic and copies ran while one was open for 0% of the time, Pallas kernels for 0%

profile of v1, /device:TPU:1, one launch (start us, length us, event | category | flops | bytes accessed | tf_op | source)
XLA Modules:
  0.0 515.4 jit_solution(15792589795778438290)
XLA Ops:
  7.2 0.0 copy-start
  7.2 0.0 reduce-scatter.2.cloned.1.call-start
  7.2 0.7 multiply_bitcast_fusion
  8.0 0.1 iota_compare_fusion.1
  8.0 0.2 copy-done
  8.2 5.8 %convolution_bitcast_fusion = f32[8,224,1024]{2,1,0:T(8,128)} fusion(bf16[8,224,128]{2,1,0:T(8,128)(2,1)S(1)} %copy-done, bf16[8,128,1024]{2,1,0:T(8,128)(2,1)} %param.4, pred[8,128]{1,0:T(8,128)(4,1)S(1)} %iota_compare_fusion.1), kind=kOutput, calls=%fused_computation.14 | convolution fusion | flops 470810624 | bytes 9896960 | tf_op jit(solution)/shard_map/tba,tan->tbn/dot_general | solution.py:44
  14.0 0.0 copy-start.4
  14.0 0.0 reduce-scatter.2.cloned.1.call-update
  14.0 0.0 all-reduce.3.cloned.1.call-start
  14.1 53.4 %reduce-scatter.2.cloned.1.call-done = f32[1,224,1024]{2,1,0:T(8,128)} async-done(((f32[8,224,1024]{2,1,0:T(8,128)}), f32[1,224,1024]{2,1,0:T(8,128)}) %reduce-scatter.2.cloned.1.call-update) | async-done | bytes 917520 | tf_op jit(solution)/shard_map/reduce_scatter | solution.py:43
  67.5 0.0 copy-done.4
  67.5 1.3 multiply_add_fusion
  68.8 0.0 copy-start.2
  68.8 4.8 convolution_convert_fusion.1
  73.6 0.0 all-reduce.3.cloned.1.call-update
  73.6 0.2 all-reduce.5.cloned.1.call-start
  73.9 149.9 %all-reduce.3.cloned.1.call-done = bf16[1024,1024]{1,0:T(8,128)(2,1)} async-done(((bf16[1024,1024]{1,0:T(8,128)(2,1)}), bf16[1024,1024]{1,0:T(8,128)(2,1)}) %all-reduce.3.cloned.1.call-update) | async-done | bytes 2097168 | tf_op jit(solution)/shard_map/psum | solution.py:57
  223.7 2.3 fusion.5
  226.8 0.0 copy-start.1
  226.8 16.3 %fusion = f32[1024,1024]{1,0:T(8,128)S(1)} fusion(bf16[1024,1024]{1,0:T(8,128)(2,1)} %all-reduce.3.cloned.1.call-done, f32[]{:T(128)S(6)} %mul.70), kind=kOutput, calls=%fused_computation.2 | convolution fusion | flops 12886999040 | bytes 6291460 | tf_op jit(solution)/shard_map/dot_general | solution.py:30
  243.2 0.0 copy-done.2
  243.2 0.0 copy-done.1
  243.2 4.1 fusion.23
  247.3 4.8 convolution_convert_fusion
  252.1 0.0 all-reduce.5.cloned.1.call-update
  252.1 151.4 %all-reduce.5.cloned.1.call-done = bf16[1024,1024]{1,0:T(8,128)(2,1)} async-done(((bf16[1024,1024]{1,0:T(8,128)(2,1)}), bf16[1024,1024]{1,0:T(8,128)(2,1)}) %all-reduce.5.cloned.1.call-update) | async-done | bytes 2097168 | tf_op jit(solution)/shard_map/psum | solution.py:57
  403.5 0.0 copy-start.3
  403.5 4.7 fusion.39
  408.2 0.0 copy-done.3
  408.2 3.7 fusion.26
  411.9 0.9 stack.3
  412.9 92.9 %all_to_all.5 = f32[8,1,224,1024]{3,2,1,0:T(8,128)S(1)} all-to-all(f32[8,1,224,1024]{3,2,1,0:T(8,128)S(1)} %stack.3), channel_id=1, replica_groups=mesh['dp'=8,'expert'=32] {'dp'}, dimensions={0} | all-to-all | bytes 14680064 | tf_op jit(solution)/shard_map/all_to_all | solution.py:21
  505.8 3.0 copy.9
Async XLA Ops:
  7.2 1.0 copy-start
  7.2 60.3 %reduce-scatter.2.cloned.1.call-start = ((), (), s32[]{:S(2)}) async-start(), calls=%async_computation.2 | async-start | bytes 8257536 | tf_op jit(solution)/shard_map/reduce_scatter | solution.py:43
  14.0 53.4 %copy-start.4 = (f32[1,224,1024]{2,1,0:T(8,128)S(1)}, f32[1,224,1024]{2,1,0:T(8,128)}, u32[]{:S(2)}) copy-start(f32[1,224,1024]{2,1,0:T(8,128)} %param.6) | copy-start | bytes 2752516
  14.0 209.7 %all-reduce.3.cloned.1.call-start = ((), (), s32[]{:S(2)}) async-start(), calls=%async_computation.3 | async-start | bytes 4194304 | tf_op jit(solution)/shard_map/psum | solution.py:57
  68.8 174.4 %copy-start.2 = (f32[1,224,1024]{2,1,0:T(8,128)}, f32[1,224,1024]{2,1,0:T(8,128)S(1)}, u32[]{:S(2)}) copy-start(f32[1,224,1024]{2,1,0:T(8,128)S(1)} %multiply_add_fusion) | copy-start | bytes 2752516
  73.6 329.9 %all-reduce.5.cloned.1.call-start = ((), (), s32[]{:S(2)}) async-start(), calls=%async_computation.4 | async-start | bytes 4194304 | tf_op jit(solution)/shard_map/psum | solution.py:57
  226.8 16.4 %copy-start.1 = (bf16[1024,1024]{1,0:T(8,128)(2,1)S(1)}, bf16[1024,1024]{1,0:T(8,128)(2,1)}, u32[]{:S(2)}) copy-start(bf16[1024,1024]{1,0:T(8,128)(2,1)} %all-reduce.3.cloned.1.call-done) | copy-start | bytes 6291460
  403.5 4.7 copy-start.3
Sparse Core Ops, SparseCore 0:
  14.2 53.2 reduce-scatter.1
  73.7 149.9 all-reduce.2
  252.2 151.2 all-reduce.4
